TPU v7x, 32 devices: a whole 2x2x4 slice. The times are simulated.
32 devices in a mesh: shot: 2 (over x), gz: 16 (over z, y, core).
Axes of the slice: x: 2, y: 2, z: 4, core: 2. Of those that a mesh axis runs over, the one named last changes fastest.
Arguments:
- source_now: float32 [256, 128, 128], P(('shot', 'gz')), parts along dimension 0, may hold values from -6 to 6
- source_before: float32 [256, 128, 128], P(('shot', 'gz')), parts along dimension 0, may hold values from -6 to 6
- receiver_now: float32 [256, 128, 128], P(('shot', 'gz')), parts along dimension 0, may hold values from -6 to 6
- receiver_before: float32 [256, 128, 128], P(('shot', 'gz')), parts along dimension 0, may hold values from -6 to 6
- speed_term: float32 [128, 128, 128], P('gz'), may hold values from 0.03 to 0.18
- saved_faces: float32 [24, 8, 128, 128], P('shot', None, 'gz'), parts along dimension 0, may hold values from -6 to 6
- face_steps: int32 [12], replicated, may hold values from 0 to 11, each once
- traces: bfloat16 [24, 128, 128], P('shot'), parts along dimension 0, may hold values from -6 to 6
- lag_offsets: int32 [8], replicated, may hold values from -8 to 8, as said below
- snap_phase: int32 [2], replicated, may hold values from 0 to 5
Outputs:
- image_out: bfloat16 [16, 128, 128, 128], P('shot', None, 'gz'), parts along dimension 0
- source_final: float32 [256, 128, 128], P(('shot', 'gz')), parts along dimension 0
- receiver_final: float32 [256, 128, 128], P(('shot', 'gz')), parts along dimension 0
There are 2 independent parts, one for each index of `shot`. A program takes and returns all parts, laid end to end along the dimension named above; an argument that names none is the same for every part. Nothing has to cross between parts.
Inputs may be any that keep to these rules, and one draw needn't show every extreme that they name: `face_steps`: each of the 12 saved slots belongs to exactly one step. `lag_offsets`: the 8 offsets are different, and both ends of the range occur.
All inputs are finite; a program needn't handle non-finite values.
Results may differ from a plain program's by a relative error of at most 0.001.
Values sent between devices are 32-bit elements; how exact they have to be, the bound alone decides.
No kernel may reach another device: no remote copies, remote signals or barrier semaphores. Data moves between devices by JAX's collectives and lax.ppermute only.
A program may use at most 64 MiB of HBM per device.

v0:
```python
import math
import jax
import jax.numpy as jnp
from jax import lax
from jax.sharding import PartitionSpec as P

LAGS = 8
LMAX = 8
SNAP_EVERY = 6
SNAPS = 2
stencil_weights = (-205.0 / 72.0, 8.0 / 5.0, -1.0 / 5.0, 8.0 / 315.0, -1.0 / 560.0)
damping = 0.25
smoothing = 16.0


def extended_2(block, sides, width):
    for axis, dim in sides:
        count = lax.axis_size(axis)
        forward = [(i, i + 1) for i in range(count - 1)]
        backward = [(target, source) for source, target in forward]
        low = lax.ppermute(
            lax.slice_in_dim(block, block.shape[dim] - width, None, axis=dim), axis, forward
        )
        high = lax.ppermute(lax.slice_in_dim(block, 0, width, axis=dim), axis, backward)
        block = jnp.concatenate([low, block, high], axis=dim)
    return block


def stencil(extended, layers):
    center = extended[:, 4 : 4 + layers]
    height = center.shape[2]
    breadth = center.shape[3]
    padded = jnp.pad(center, ((0, 0), (0, 0), (4, 4), (4, 4)))
    summed = 3.0 * stencil_weights[0] * center
    for offset in range(1, 5):
        weight = stencil_weights[offset]
        summed = summed + weight * (
            extended[:, 4 + offset : 4 + offset + layers]
            + extended[:, 4 - offset : 4 - offset + layers]
        )
        summed = summed + weight * (
            padded[:, :, 4 + offset : 4 + offset + height, 4 : 4 + breadth]
            + padded[:, :, 4 - offset : 4 - offset + height, 4 : 4 + breadth]
        )
        summed = summed + weight * (
            padded[:, :, 4 : 4 + height, 4 + offset : 4 + offset + breadth]
            + padded[:, :, 4 : 4 + height, 4 - offset : 4 - offset + breadth]
        )
    return summed


def advance(extended, center, previous, speed_term, faces_now, trace_now, top_row, layers):
    updated = 2.0 * center - previous + speed_term * stencil(extended, layers)
    breadth = updated.shape[3]
    column = lax.broadcasted_iota(jnp.int32, (8, breadth), 1)
    which = lax.broadcasted_iota(jnp.int32, (8, breadth), 0)
    target = jnp.where(which < 4, which, which + breadth - 8)
    placing = (column == target).astype(jnp.float32)
    boundary = jnp.einsum("fzy,fx->zyx", faces_now, placing, precision=lax.Precision.HIGHEST)
    x_index = lax.broadcasted_iota(jnp.int32, (1, 1, breadth), 2)
    edge_mask = (x_index < 4) | (x_index >= breadth - 4)
    source = jnp.where(edge_mask, boundary, updated[0])
    top_mask = lax.broadcasted_iota(jnp.int32, (layers, 1, 1), 0) == top_row
    receiver = updated[1] + jnp.where(top_mask, trace_now[None], 0.0)
    return jnp.stack([source, receiver])


def lag_images(snapshot, lag_offsets):
    source = snapshot[0]
    receiver = snapshot[1]
    margin = ((0, 0), (0, 0), (LMAX, LMAX))
    source_pad = jnp.pad(source, margin)
    receiver_pad = jnp.pad(receiver, margin)
    breadth = source.shape[2]
    images = []
    for lag_index in range(LAGS):
        lag_now = lag_offsets[lag_index]
        shifted_source = lax.dynamic_slice_in_dim(source_pad, LMAX - lag_now, breadth, 2)
        shifted_receiver = lax.dynamic_slice_in_dim(receiver_pad, LMAX + lag_now, breadth, 2)
        images.append(shifted_source * shifted_receiver)
    return (jnp.stack(images), source * source)


def depth_inverse(layers):
    ratio = (1.0 + 2.0 * smoothing) / (2.0 * smoothing)
    theta = math.log(ratio + math.sqrt(ratio * ratio - 1.0))
    hyper_sine = 0.5 * (math.exp(theta) - math.exp(-theta))
    scale = 1.0 / (2.0 * smoothing * hyper_sine * (1.0 - math.exp(-2.0 * (layers + 1) * theta)))
    row_index = lax.broadcasted_iota(jnp.int32, (layers, layers), 0)
    col_index = lax.broadcasted_iota(jnp.int32, (layers, layers), 1)
    apart = jnp.abs(row_index - col_index).astype(jnp.float32)
    joined = (row_index + col_index).astype(jnp.float32)
    total = float(layers)
    green = (
        jnp.exp(-theta * apart)
        - jnp.exp(-theta * (2.0 * total - joined))
        - jnp.exp(-theta * (joined + 2.0))
        + jnp.exp(-theta * (2.0 * total + 2.0 - apart))
    )
    return green * scale


def finish(raw_image, illumination):
    layers = illumination.shape[0]
    columns = illumination.reshape(layers, -1)
    inverse = depth_inverse(layers)
    smooth = jnp.dot(
        inverse, columns, precision=lax.Precision.HIGHEST, preferred_element_type=jnp.float32
    ).reshape(illumination.shape)
    return (raw_image / (smooth + damping)).astype(jnp.bfloat16)


def local(
    source_now,
    source_before,
    receiver_now,
    receiver_before,
    speed_term,
    saved_faces,
    face_steps,
    traces,
    lag_offsets,
    snap_phase,
):
    current = jnp.stack([source_now, receiver_now])
    previous = jnp.stack([source_before, receiver_before])
    layers = source_now.shape[0]
    is_top = lax.axis_index("gz") == 0
    top_row = jnp.where(is_top, 0, -1)
    raw_image = jnp.zeros((1,), jnp.float32)
    illumination = jnp.zeros((1,), jnp.float32)
    for window in range(SNAPS):
        phase_now = snap_phase[window]
        empty_snapshot = jnp.zeros_like(current)

        def one_step(local_index, carried):
            current, previous, snapshot = carried
            step_index = window * SNAP_EVERY + local_index
            extended = extended_2(current, (("gz", 1),), 4)
            faces_now = lax.dynamic_index_in_dim(
                saved_faces, face_steps[step_index], 0, keepdims=False
            )
            trace_now = lax.dynamic_index_in_dim(traces, step_index, 0, keepdims=False).astype(
                jnp.float32
            )
            updated = advance(
                extended, current, previous, speed_term, faces_now, trace_now, top_row, layers
            )
            snapshot = jnp.where(local_index == phase_now, updated, snapshot)
            return (updated, current, snapshot)

        current, previous, snapshot = lax.fori_loop(
            0, SNAP_EVERY, one_step, (current, previous, empty_snapshot)
        )
        columns_now = lax.all_to_all(snapshot, "gz", split_axis=2, concat_axis=1, tiled=True)
        raw_now, light_now = lag_images(columns_now, lag_offsets)
        if window == 0:
            raw_image = raw_now
            illumination = light_now
        else:
            raw_image = raw_image + raw_now
            illumination = illumination + light_now
    return (finish(raw_image, illumination), current[0], current[1])


def solution(mesh):
    return jax.shard_map(
        local,
        mesh=mesh,
        in_specs=(
            P(("shot", "gz"), None, None),
            P(("shot", "gz"), None, None),
            P(("shot", "gz"), None, None),
            P(("shot", "gz"), None, None),
            P("gz", None, None),
            P("shot", None, "gz", None),
            P(),
            P("shot", None, None),
            P(),
            P(),
        ),
        out_specs=(
            P("shot", None, "gz", None),
            P(("shot", "gz"), None, None),
            P(("shot", "gz"), None, None),
        ),
        check_vma=False,
    )
```

profile of v0, /device:TPU:9, one launch (start us, length us, event | category | flops | bytes accessed | tf_op | source)
XLA Modules:
  0.0 345.8 jit_solution(5449457502616833850)
XLA Ops:
  5.8 135.9 %while.44 = (s32[]{:T(128)}, f32[2,8,128,128]{3,2,1,0:T(8,128)S(1)}, f32[2,8,128,128]{3,2,1,0:T(8,128)S(1)}, f32[2,8,128,128]{3,2,1,0:T(8,128)}, s32[12]{0:T(128...) while((s32[]{:T(128)}, ...), condition=%wide.region_1.2_spmd.clone, body=%wide.region_0.1_spmd.clone.sunk | while | flops 24529312 | bytes 40568852 | solution.py:152
  6.8 3.7 %collective-permute-start = (f32[2,4,128,128]{3,2,1,0:T(8,128)}, f32[2,4,128,128]{3,2,1,0:T(8,128)}, u32[]{:S(2)}, u32[]{:S(2)}) collective-permute-start(f32[2,4,128,128]{3,2,1,0:T(8,128)} %get-tuple-element.965), channel_id=1, source_target_pairs={{0,1},{1,2},{2,3},{3,4},{4,5},{5,6},{6,7},{7,8},{8,9},{9,10},{10,1... | collective-permute-start | bytes 1572872 | tf_op jit(solution)/shard_map/while/body/eval_jaxpr/ppermute | solution.py:21
  10.5 1.9 collective-permute-start.1
  16.4 6.2 %collective-permute-done = f32[2,4,128,128]{3,2,1,0:T(8,128)} collective-permute-done((f32[2,4,128,128]{3,2,1,0:T(8,128)}, f32[2,4,128,128]{3,2,1,0:T(8,128)}, u32[]{:S(2)}, u32[]{:S(2)}) %collective-permute-start) | collective-permute-done | bytes 524320 | tf_op jit(solution)/shard_map/while/body/eval_jaxpr/ppermute | solution.py:21
  24.1 2.4 fusion.183
  30.2 4.3 %collective-permute-start = (f32[2,4,128,128]{3,2,1,0:T(8,128)}, f32[2,4,128,128]{3,2,1,0:T(8,128)}, u32[]{:S(2)}, u32[]{:S(2)}) collective-permute-start(f32[2,4,128,128]{3,2,1,0:T(8,128)} %get-tuple-element.965), channel_id=1, source_target_pairs={{0,1},{1,2},{2,3},{3,4},{4,5},{5,6},{6,7},{7,8},{8,9},{9,10},{10,1... | collective-permute-start | bytes 1572872 | tf_op jit(solution)/shard_map/while/body/eval_jaxpr/ppermute | solution.py:21
  34.4 1.9 collective-permute-start.1
  40.2 6.2 %collective-permute-done = f32[2,4,128,128]{3,2,1,0:T(8,128)} collective-permute-done((f32[2,4,128,128]{3,2,1,0:T(8,128)}, f32[2,4,128,128]{3,2,1,0:T(8,128)}, u32[]{:S(2)}, u32[]{:S(2)}) %collective-permute-start) | collective-permute-done | bytes 524320 | tf_op jit(solution)/shard_map/while/body/eval_jaxpr/ppermute | solution.py:21
  47.8 2.4 fusion.183
  53.9 4.4 %collective-permute-start = (f32[2,4,128,128]{3,2,1,0:T(8,128)}, f32[2,4,128,128]{3,2,1,0:T(8,128)}, u32[]{:S(2)}, u32[]{:S(2)}) collective-permute-start(f32[2,4,128,128]{3,2,1,0:T(8,128)} %get-tuple-element.965), channel_id=1, source_target_pairs={{0,1},{1,2},{2,3},{3,4},{4,5},{5,6},{6,7},{7,8},{8,9},{9,10},{10,1... | collective-permute-start | bytes 1572872 | tf_op jit(solution)/shard_map/while/body/eval_jaxpr/ppermute | solution.py:21
  58.3 1.9 collective-permute-start.1
  64.1 6.2 %collective-permute-done = f32[2,4,128,128]{3,2,1,0:T(8,128)} collective-permute-done((f32[2,4,128,128]{3,2,1,0:T(8,128)}, f32[2,4,128,128]{3,2,1,0:T(8,128)}, u32[]{:S(2)}, u32[]{:S(2)}) %collective-permute-start) | collective-permute-done | bytes 524320 | tf_op jit(solution)/shard_map/while/body/eval_jaxpr/ppermute | solution.py:21
  71.7 2.4 fusion.183
  77.8 4.4 %collective-permute-start = (f32[2,4,128,128]{3,2,1,0:T(8,128)}, f32[2,4,128,128]{3,2,1,0:T(8,128)}, u32[]{:S(2)}, u32[]{:S(2)}) collective-permute-start(f32[2,4,128,128]{3,2,1,0:T(8,128)} %get-tuple-element.965), channel_id=1, source_target_pairs={{0,1},{1,2},{2,3},{3,4},{4,5},{5,6},{6,7},{7,8},{8,9},{9,10},{10,1... | collective-permute-start | bytes 1572872 | tf_op jit(solution)/shard_map/while/body/eval_jaxpr/ppermute | solution.py:21
  82.2 1.9 collective-permute-start.1
  88.0 4.7 %collective-permute-done = f32[2,4,128,128]{3,2,1,0:T(8,128)} collective-permute-done((f32[2,4,128,128]{3,2,1,0:T(8,128)}, f32[2,4,128,128]{3,2,1,0:T(8,128)}, u32[]{:S(2)}, u32[]{:S(2)}) %collective-permute-start) | collective-permute-done | bytes 524320 | tf_op jit(solution)/shard_map/while/body/eval_jaxpr/ppermute | solution.py:21
  94.1 2.4 fusion.183
  100.1 4.4 %collective-permute-start = (f32[2,4,128,128]{3,2,1,0:T(8,128)}, f32[2,4,128,128]{3,2,1,0:T(8,128)}, u32[]{:S(2)}, u32[]{:S(2)}) collective-permute-start(f32[2,4,128,128]{3,2,1,0:T(8,128)} %get-tuple-element.965), channel_id=1, source_target_pairs={{0,1},{1,2},{2,3},{3,4},{4,5},{5,6},{6,7},{7,8},{8,9},{9,10},{10,1... | collective-permute-start | bytes 1572872 | tf_op jit(solution)/shard_map/while/body/eval_jaxpr/ppermute | solution.py:21
  104.5 1.9 collective-permute-start.1
  110.3 3.7 %collective-permute-done = f32[2,4,128,128]{3,2,1,0:T(8,128)} collective-permute-done((f32[2,4,128,128]{3,2,1,0:T(8,128)}, f32[2,4,128,128]{3,2,1,0:T(8,128)}, u32[]{:S(2)}, u32[]{:S(2)}) %collective-permute-start) | collective-permute-done | bytes 524320 | tf_op jit(solution)/shard_map/while/body/eval_jaxpr/ppermute | solution.py:21
  115.4 2.4 fusion.183
  121.5 4.4 %collective-permute-start = (f32[2,4,128,128]{3,2,1,0:T(8,128)}, f32[2,4,128,128]{3,2,1,0:T(8,128)}, u32[]{:S(2)}, u32[]{:S(2)}) collective-permute-start(f32[2,4,128,128]{3,2,1,0:T(8,128)} %get-tuple-element.965), channel_id=1, source_target_pairs={{0,1},{1,2},{2,3},{3,4},{4,5},{5,6},{6,7},{7,8},{8,9},{9,10},{10,1... | collective-permute-start | bytes 1572872 | tf_op jit(solution)/shard_map/while/body/eval_jaxpr/ppermute | solution.py:21
  125.9 1.9 collective-permute-start.1
  131.7 3.6 %collective-permute-done = f32[2,4,128,128]{3,2,1,0:T(8,128)} collective-permute-done((f32[2,4,128,128]{3,2,1,0:T(8,128)}, f32[2,4,128,128]{3,2,1,0:T(8,128)}, u32[]{:S(2)}, u32[]{:S(2)}) %collective-permute-start) | collective-permute-done | bytes 524320 | tf_op jit(solution)/shard_map/while/body/eval_jaxpr/ppermute | solution.py:21
  136.6 2.4 fusion.183
  141.6 128.2 %while.45 = (s32[]{:T(128)}, f32[2,8,128,128]{3,2,1,0:T(8,128)S(1)}, f32[2,8,128,128]{3,2,1,0:T(8,128)S(1)}, f32[2,8,128,128]{3,2,1,0:T(8,128)}, s32[12]{0:T(128...) while((s32[]{:T(128)}, ...), condition=%wide.region_3.4_spmd.clone, body=%wide.region_2.3_spmd.clone.sunk | while | flops 24529316 | bytes 40568908 | solution.py:152
  142.7 4.4 %collective-permute-start.2 = (f32[2,4,128,128]{3,2,1,0:T(8,128)}, f32[2,4,128,128]{3,2,1,0:T(8,128)}, u32[]{:S(2)}, u32[]{:S(2)}) collective-permute-start(f32[2,4,128,128]{3,2,1,0:T(8,128)} %get-tuple-element.981), channel_id=1, source_target_pairs={{0,1},{1,2},{2,3},{3,4},{4,5},{5,6},{6,7},{7,8},{8,9},{9,10},{10,1... | collective-permute-start | bytes 1572872 | tf_op jit(solution)/shard_map/while/body/eval_jaxpr/ppermute | solution.py:21
  153.0 3.6 %collective-permute-done.2 = f32[2,4,128,128]{3,2,1,0:T(8,128)} collective-permute-done((f32[2,4,128,128]{3,2,1,0:T(8,128)}, f32[2,4,128,128]{3,2,1,0:T(8,128)}, u32[]{:S(2)}, u32[]{:S(2)}) %collective-permute-start.2) | collective-permute-done | bytes 524320 | tf_op jit(solution)/shard_map/while/body/eval_jaxpr/ppermute | solution.py:21
  158.0 2.4 fusion.188
  164.1 4.4 %collective-permute-start.2 = (f32[2,4,128,128]{3,2,1,0:T(8,128)}, f32[2,4,128,128]{3,2,1,0:T(8,128)}, u32[]{:S(2)}, u32[]{:S(2)}) collective-permute-start(f32[2,4,128,128]{3,2,1,0:T(8,128)} %get-tuple-element.981), channel_id=1, source_target_pairs={{0,1},{1,2},{2,3},{3,4},{4,5},{5,6},{6,7},{7,8},{8,9},{9,10},{10,1... | collective-permute-start | bytes 1572872 | tf_op jit(solution)/shard_map/while/body/eval_jaxpr/ppermute | solution.py:21
  174.4 3.6 %collective-permute-done.2 = f32[2,4,128,128]{3,2,1,0:T(8,128)} collective-permute-done((f32[2,4,128,128]{3,2,1,0:T(8,128)}, f32[2,4,128,128]{3,2,1,0:T(8,128)}, u32[]{:S(2)}, u32[]{:S(2)}) %collective-permute-start.2) | collective-permute-done | bytes 524320 | tf_op jit(solution)/shard_map/while/body/eval_jaxpr/ppermute | solution.py:21
  179.3 2.4 fusion.188
  185.4 4.4 %collective-permute-start.2 = (f32[2,4,128,128]{3,2,1,0:T(8,128)}, f32[2,4,128,128]{3,2,1,0:T(8,128)}, u32[]{:S(2)}, u32[]{:S(2)}) collective-permute-start(f32[2,4,128,128]{3,2,1,0:T(8,128)} %get-tuple-element.981), channel_id=1, source_target_pairs={{0,1},{1,2},{2,3},{3,4},{4,5},{5,6},{6,7},{7,8},{8,9},{9,10},{10,1... | collective-permute-start | bytes 1572872 | tf_op jit(solution)/shard_map/while/body/eval_jaxpr/ppermute | solution.py:21
  195.7 3.6 %collective-permute-done.2 = f32[2,4,128,128]{3,2,1,0:T(8,128)} collective-permute-done((f32[2,4,128,128]{3,2,1,0:T(8,128)}, f32[2,4,128,128]{3,2,1,0:T(8,128)}, u32[]{:S(2)}, u32[]{:S(2)}) %collective-permute-start.2) | collective-permute-done | bytes 524320 | tf_op jit(solution)/shard_map/while/body/eval_jaxpr/ppermute | solution.py:21
  200.7 2.4 fusion.188
  206.8 4.4 %collective-permute-start.2 = (f32[2,4,128,128]{3,2,1,0:T(8,128)}, f32[2,4,128,128]{3,2,1,0:T(8,128)}, u32[]{:S(2)}, u32[]{:S(2)}) collective-permute-start(f32[2,4,128,128]{3,2,1,0:T(8,128)} %get-tuple-element.981), channel_id=1, source_target_pairs={{0,1},{1,2},{2,3},{3,4},{4,5},{5,6},{6,7},{7,8},{8,9},{9,10},{10,1... | collective-permute-start | bytes 1572872 | tf_op jit(solution)/shard_map/while/body/eval_jaxpr/ppermute | solution.py:21
  217.1 3.6 %collective-permute-done.2 = f32[2,4,128,128]{3,2,1,0:T(8,128)} collective-permute-done((f32[2,4,128,128]{3,2,1,0:T(8,128)}, f32[2,4,128,128]{3,2,1,0:T(8,128)}, u32[]{:S(2)}, u32[]{:S(2)}) %collective-permute-start.2) | collective-permute-done | bytes 524320 | tf_op jit(solution)/shard_map/while/body/eval_jaxpr/ppermute | solution.py:21
  222.0 2.4 fusion.188
  228.1 4.4 %collective-permute-start.2 = (f32[2,4,128,128]{3,2,1,0:T(8,128)}, f32[2,4,128,128]{3,2,1,0:T(8,128)}, u32[]{:S(2)}, u32[]{:S(2)}) collective-permute-start(f32[2,4,128,128]{3,2,1,0:T(8,128)} %get-tuple-element.981), channel_id=1, source_target_pairs={{0,1},{1,2},{2,3},{3,4},{4,5},{5,6},{6,7},{7,8},{8,9},{9,10},{10,1... | collective-permute-start | bytes 1572872 | tf_op jit(solution)/shard_map/while/body/eval_jaxpr/ppermute | solution.py:21
  238.4 3.6 %collective-permute-done.2 = f32[2,4,128,128]{3,2,1,0:T(8,128)} collective-permute-done((f32[2,4,128,128]{3,2,1,0:T(8,128)}, f32[2,4,128,128]{3,2,1,0:T(8,128)}, u32[]{:S(2)}, u32[]{:S(2)}) %collective-permute-start.2) | collective-permute-done | bytes 524320 | tf_op jit(solution)/shard_map/while/body/eval_jaxpr/ppermute | solution.py:21
  243.4 2.4 fusion.188
  249.5 4.4 %collective-permute-start.2 = (f32[2,4,128,128]{3,2,1,0:T(8,128)}, f32[2,4,128,128]{3,2,1,0:T(8,128)}, u32[]{:S(2)}, u32[]{:S(2)}) collective-permute-start(f32[2,4,128,128]{3,2,1,0:T(8,128)} %get-tuple-element.981), channel_id=1, source_target_pairs={{0,1},{1,2},{2,3},{3,4},{4,5},{5,6},{6,7},{7,8},{8,9},{9,10},{10,1... | collective-permute-start | bytes 1572872 | tf_op jit(solution)/shard_map/while/body/eval_jaxpr/ppermute | solution.py:21
  259.8 3.6 %collective-permute-done.2 = f32[2,4,128,128]{3,2,1,0:T(8,128)} collective-permute-done((f32[2,4,128,128]{3,2,1,0:T(8,128)}, f32[2,4,128,128]{3,2,1,0:T(8,128)}, u32[]{:S(2)}, u32[]{:S(2)}) %collective-permute-start.2) | collective-permute-done | bytes 524320 | tf_op jit(solution)/shard_map/while/body/eval_jaxpr/ppermute | solution.py:21
  264.8 2.4 fusion.188
  269.8 2.9 copy.32
  272.7 8.0 %all-to-all-start.1 = ((f32[2,8,128,128]{3,1,0,2:T(8,128)}), f32[2,8,128,128]{3,1,0,2:T(8,128)S(1)}, u32[]{:S(2)}, u32[]{:S(2)}) async-start(f32[2,8,128,128]{3,1,0,2:T(8,128)} %copy.32), calls=%async_computation.1 | async-start | bytes 2097152 | tf_op jit(solution)/shard_map/all_to_all | solution.py:155
  282.3 23.3 %all-to-all-done.1 = f32[2,8,128,128]{3,1,0,2:T(8,128)S(1)} async-done(((f32[2,8,128,128]{3,1,0,2:T(8,128)}), f32[2,8,128,128]{3,1,0,2:T(8,128)S(1)}, u32[]{:S(2)}, u32[]{:S(2)}) %all-to-all-start.1) | async-done | bytes 1048608 | tf_op jit(solution)/shard_map/all_to_all | solution.py:155
  305.6 4.8 %all-to-all-start = ((f32[2,8,128,128]{3,1,0,2:T(8,128)}), f32[2,8,128,128]{3,1,0,2:T(8,128)S(1)}, u32[]{:S(2)}, u32[]{:S(2)}) async-start(f32[2,8,128,128]{3,1,0,2:T(8,128)} %copy.29), calls=%async_computation | async-start | bytes 2097152 | tf_op jit(solution)/shard_map/all_to_all | solution.py:155
  (275 shorter events, 109.5 us)
Async XLA Ops:
  0.6 5.1 %copy-start.7 = (s32[12]{0:T(128)S(1)}, s32[12]{0:T(128)}, u32[]{:S(2)}) copy-start(s32[12]{0:T(128)} %param.20) | copy-start | bytes 148
  0.6 5.1 %copy-start = (f32[8,128,128]{2,1,0:T(8,128)S(1)}, f32[8,128,128]{2,1,0:T(8,128)}, u32[]{:S(2)}) copy-start(f32[8,128,128]{2,1,0:T(8,128)} %param.18) | copy-start | bytes 1572868
  6.8 15.7 %collective-permute-start = (f32[2,4,128,128]{3,2,1,0:T(8,128)}, f32[2,4,128,128]{3,2,1,0:T(8,128)}, u32[]{:S(2)}, u32[]{:S(2)}) collective-permute-start(f32[2,4,128,128]{3,2,1,0:T(8,128)} %get-tuple-element.965), channel_id=1, source_target_pairs={{0,1},{1,2},{2,3},{3,4},{4,5},{5,6},{6,7},{7,8},{8,9},{9,10},{10,1... | collective-permute-start | bytes 1572872 | tf_op jit(solution)/shard_map/while/body/eval_jaxpr/ppermute | solution.py:21
  10.5 13.5 %collective-permute-start.1 = (f32[2,4,128,128]{3,2,1,0:T(8,128)}, f32[2,4,128,128]{3,2,1,0:T(8,128)S(1)}, u32[]{:S(2)}, u32[]{:S(2)}) collective-permute-start(f32[2,4,128,128]{3,2,1,0:T(8,128)} %get-tuple-element.968), channel_id=1, source_target_pairs={{1,0},{2,1},{3,2},{4,3},{5,4},{6,5},{7,6},{8,7},{9,8},{10,9},{11,1... | collective-permute-start | bytes 1572872 | tf_op jit(solution)/shard_map/while/body/eval_jaxpr/ppermute | solution.py:24
  26.5 1.2 copy-start.3
  30.2 16.3 %collective-permute-start = (f32[2,4,128,128]{3,2,1,0:T(8,128)}, f32[2,4,128,128]{3,2,1,0:T(8,128)}, u32[]{:S(2)}, u32[]{:S(2)}) collective-permute-start(f32[2,4,128,128]{3,2,1,0:T(8,128)} %get-tuple-element.965), channel_id=1, source_target_pairs={{0,1},{1,2},{2,3},{3,4},{4,5},{5,6},{6,7},{7,8},{8,9},{9,10},{10,1... | collective-permute-start | bytes 1572872 | tf_op jit(solution)/shard_map/while/body/eval_jaxpr/ppermute | solution.py:21
  34.4 13.4 %collective-permute-start.1 = (f32[2,4,128,128]{3,2,1,0:T(8,128)}, f32[2,4,128,128]{3,2,1,0:T(8,128)S(1)}, u32[]{:S(2)}, u32[]{:S(2)}) collective-permute-start(f32[2,4,128,128]{3,2,1,0:T(8,128)} %get-tuple-element.968), channel_id=1, source_target_pairs={{1,0},{2,1},{3,2},{4,3},{5,4},{6,5},{7,6},{8,7},{9,8},{10,9},{11,1... | collective-permute-start | bytes 1572872 | tf_op jit(solution)/shard_map/while/body/eval_jaxpr/ppermute | solution.py:24
  50.2 1.2 copy-start.3
  53.9 16.4 %collective-permute-start = (f32[2,4,128,128]{3,2,1,0:T(8,128)}, f32[2,4,128,128]{3,2,1,0:T(8,128)}, u32[]{:S(2)}, u32[]{:S(2)}) collective-permute-start(f32[2,4,128,128]{3,2,1,0:T(8,128)} %get-tuple-element.965), channel_id=1, source_target_pairs={{0,1},{1,2},{2,3},{3,4},{4,5},{5,6},{6,7},{7,8},{8,9},{9,10},{10,1... | collective-permute-start | bytes 1572872 | tf_op jit(solution)/shard_map/while/body/eval_jaxpr/ppermute | solution.py:21
  58.3 13.4 %collective-permute-start.1 = (f32[2,4,128,128]{3,2,1,0:T(8,128)}, f32[2,4,128,128]{3,2,1,0:T(8,128)S(1)}, u32[]{:S(2)}, u32[]{:S(2)}) collective-permute-start(f32[2,4,128,128]{3,2,1,0:T(8,128)} %get-tuple-element.968), channel_id=1, source_target_pairs={{1,0},{2,1},{3,2},{4,3},{5,4},{6,5},{7,6},{8,7},{9,8},{10,9},{11,1... | collective-permute-start | bytes 1572872 | tf_op jit(solution)/shard_map/while/body/eval_jaxpr/ppermute | solution.py:24
  74.1 1.2 copy-start.3
  77.8 14.9 %collective-permute-start = (f32[2,4,128,128]{3,2,1,0:T(8,128)}, f32[2,4,128,128]{3,2,1,0:T(8,128)}, u32[]{:S(2)}, u32[]{:S(2)}) collective-permute-start(f32[2,4,128,128]{3,2,1,0:T(8,128)} %get-tuple-element.965), channel_id=1, source_target_pairs={{0,1},{1,2},{2,3},{3,4},{4,5},{5,6},{6,7},{7,8},{8,9},{9,10},{10,1... | collective-permute-start | bytes 1572872 | tf_op jit(solution)/shard_map/while/body/eval_jaxpr/ppermute | solution.py:21
  82.2 11.8 %collective-permute-start.1 = (f32[2,4,128,128]{3,2,1,0:T(8,128)}, f32[2,4,128,128]{3,2,1,0:T(8,128)S(1)}, u32[]{:S(2)}, u32[]{:S(2)}) collective-permute-start(f32[2,4,128,128]{3,2,1,0:T(8,128)} %get-tuple-element.968), channel_id=1, source_target_pairs={{1,0},{2,1},{3,2},{4,3},{5,4},{6,5},{7,6},{8,7},{9,8},{10,9},{11,1... | collective-permute-start | bytes 1572872 | tf_op jit(solution)/shard_map/while/body/eval_jaxpr/ppermute | solution.py:24
  96.5 1.2 copy-start.3
  100.1 13.9 %collective-permute-start = (f32[2,4,128,128]{3,2,1,0:T(8,128)}, f32[2,4,128,128]{3,2,1,0:T(8,128)}, u32[]{:S(2)}, u32[]{:S(2)}) collective-permute-start(f32[2,4,128,128]{3,2,1,0:T(8,128)} %get-tuple-element.965), channel_id=1, source_target_pairs={{0,1},{1,2},{2,3},{3,4},{4,5},{5,6},{6,7},{7,8},{8,9},{9,10},{10,1... | collective-permute-start | bytes 1572872 | tf_op jit(solution)/shard_map/while/body/eval_jaxpr/ppermute | solution.py:21
  104.5 10.8 %collective-permute-start.1 = (f32[2,4,128,128]{3,2,1,0:T(8,128)}, f32[2,4,128,128]{3,2,1,0:T(8,128)S(1)}, u32[]{:S(2)}, u32[]{:S(2)}) collective-permute-start(f32[2,4,128,128]{3,2,1,0:T(8,128)} %get-tuple-element.968), channel_id=1, source_target_pairs={{1,0},{2,1},{3,2},{4,3},{5,4},{6,5},{7,6},{8,7},{9,8},{10,9},{11,1... | collective-permute-start | bytes 1572872 | tf_op jit(solution)/shard_map/while/body/eval_jaxpr/ppermute | solution.py:24
  117.8 1.2 copy-start.3
  121.5 13.8 %collective-permute-start = (f32[2,4,128,128]{3,2,1,0:T(8,128)}, f32[2,4,128,128]{3,2,1,0:T(8,128)}, u32[]{:S(2)}, u32[]{:S(2)}) collective-permute-start(f32[2,4,128,128]{3,2,1,0:T(8,128)} %get-tuple-element.965), channel_id=1, source_target_pairs={{0,1},{1,2},{2,3},{3,4},{4,5},{5,6},{6,7},{7,8},{8,9},{9,10},{10,1... | collective-permute-start | bytes 1572872 | tf_op jit(solution)/shard_map/while/body/eval_jaxpr/ppermute | solution.py:21
  125.9 10.7 %collective-permute-start.1 = (f32[2,4,128,128]{3,2,1,0:T(8,128)}, f32[2,4,128,128]{3,2,1,0:T(8,128)S(1)}, u32[]{:S(2)}, u32[]{:S(2)}) collective-permute-start(f32[2,4,128,128]{3,2,1,0:T(8,128)} %get-tuple-element.968), channel_id=1, source_target_pairs={{1,0},{2,1},{3,2},{4,3},{5,4},{6,5},{7,6},{8,7},{9,8},{10,9},{11,1... | collective-permute-start | bytes 1572872 | tf_op jit(solution)/shard_map/while/body/eval_jaxpr/ppermute | solution.py:24
  139.1 1.2 copy-start.3
  142.7 13.9 %collective-permute-start.2 = (f32[2,4,128,128]{3,2,1,0:T(8,128)}, f32[2,4,128,128]{3,2,1,0:T(8,128)}, u32[]{:S(2)}, u32[]{:S(2)}) collective-permute-start(f32[2,4,128,128]{3,2,1,0:T(8,128)} %get-tuple-element.981), channel_id=1, source_target_pairs={{0,1},{1,2},{2,3},{3,4},{4,5},{5,6},{6,7},{7,8},{8,9},{9,10},{10,1... | collective-permute-start | bytes 1572872 | tf_op jit(solution)/shard_map/while/body/eval_jaxpr/ppermute | solution.py:21
  147.1 10.8 %collective-permute-start.3 = (f32[2,4,128,128]{3,2,1,0:T(8,128)}, f32[2,4,128,128]{3,2,1,0:T(8,128)S(1)}, u32[]{:S(2)}, u32[]{:S(2)}) collective-permute-start(f32[2,4,128,128]{3,2,1,0:T(8,128)} %get-tuple-element.984), channel_id=1, source_target_pairs={{1,0},{2,1},{3,2},{4,3},{5,4},{6,5},{7,6},{8,7},{9,8},{10,9},{11,1... | collective-permute-start | bytes 1572872 | tf_op jit(solution)/shard_map/while/body/eval_jaxpr/ppermute | solution.py:24
  160.4 1.2 copy-start.1
  162.0 1.0 copy-start.2
  164.1 13.8 %collective-permute-start.2 = (f32[2,4,128,128]{3,2,1,0:T(8,128)}, f32[2,4,128,128]{3,2,1,0:T(8,128)}, u32[]{:S(2)}, u32[]{:S(2)}) collective-permute-start(f32[2,4,128,128]{3,2,1,0:T(8,128)} %get-tuple-element.981), channel_id=1, source_target_pairs={{0,1},{1,2},{2,3},{3,4},{4,5},{5,6},{6,7},{7,8},{8,9},{9,10},{10,1... | collective-permute-start | bytes 1572872 | tf_op jit(solution)/shard_map/while/body/eval_jaxpr/ppermute | solution.py:21
  168.5 10.8 %collective-permute-start.3 = (f32[2,4,128,128]{3,2,1,0:T(8,128)}, f32[2,4,128,128]{3,2,1,0:T(8,128)S(1)}, u32[]{:S(2)}, u32[]{:S(2)}) collective-permute-start(f32[2,4,128,128]{3,2,1,0:T(8,128)} %get-tuple-element.984), channel_id=1, source_target_pairs={{1,0},{2,1},{3,2},{4,3},{5,4},{6,5},{7,6},{8,7},{9,8},{10,9},{11,1... | collective-permute-start | bytes 1572872 | tf_op jit(solution)/shard_map/while/body/eval_jaxpr/ppermute | solution.py:24
  181.7 1.2 copy-start.1
  183.3 1.0 copy-start.2
  185.4 13.9 %collective-permute-start.2 = (f32[2,4,128,128]{3,2,1,0:T(8,128)}, f32[2,4,128,128]{3,2,1,0:T(8,128)}, u32[]{:S(2)}, u32[]{:S(2)}) collective-permute-start(f32[2,4,128,128]{3,2,1,0:T(8,128)} %get-tuple-element.981), channel_id=1, source_target_pairs={{0,1},{1,2},{2,3},{3,4},{4,5},{5,6},{6,7},{7,8},{8,9},{9,10},{10,1... | collective-permute-start | bytes 1572872 | tf_op jit(solution)/shard_map/while/body/eval_jaxpr/ppermute | solution.py:21
  189.8 10.8 %collective-permute-start.3 = (f32[2,4,128,128]{3,2,1,0:T(8,128)}, f32[2,4,128,128]{3,2,1,0:T(8,128)S(1)}, u32[]{:S(2)}, u32[]{:S(2)}) collective-permute-start(f32[2,4,128,128]{3,2,1,0:T(8,128)} %get-tuple-element.984), channel_id=1, source_target_pairs={{1,0},{2,1},{3,2},{4,3},{5,4},{6,5},{7,6},{8,7},{9,8},{10,9},{11,1... | collective-permute-start | bytes 1572872 | tf_op jit(solution)/shard_map/while/body/eval_jaxpr/ppermute | solution.py:24
  203.1 1.2 copy-start.1
  204.7 1.0 copy-start.2
  206.8 13.8 %collective-permute-start.2 = (f32[2,4,128,128]{3,2,1,0:T(8,128)}, f32[2,4,128,128]{3,2,1,0:T(8,128)}, u32[]{:S(2)}, u32[]{:S(2)}) collective-permute-start(f32[2,4,128,128]{3,2,1,0:T(8,128)} %get-tuple-element.981), channel_id=1, source_target_pairs={{0,1},{1,2},{2,3},{3,4},{4,5},{5,6},{6,7},{7,8},{8,9},{9,10},{10,1... | collective-permute-start | bytes 1572872 | tf_op jit(solution)/shard_map/while/body/eval_jaxpr/ppermute | solution.py:21
  211.2 10.8 %collective-permute-start.3 = (f32[2,4,128,128]{3,2,1,0:T(8,128)}, f32[2,4,128,128]{3,2,1,0:T(8,128)S(1)}, u32[]{:S(2)}, u32[]{:S(2)}) collective-permute-start(f32[2,4,128,128]{3,2,1,0:T(8,128)} %get-tuple-element.984), channel_id=1, source_target_pairs={{1,0},{2,1},{3,2},{4,3},{5,4},{6,5},{7,6},{8,7},{9,8},{10,9},{11,1... | collective-permute-start | bytes 1572872 | tf_op jit(solution)/shard_map/while/body/eval_jaxpr/ppermute | solution.py:24
  224.5 1.2 copy-start.1
  226.1 1.0 copy-start.2
  228.1 13.9 %collective-permute-start.2 = (f32[2,4,128,128]{3,2,1,0:T(8,128)}, f32[2,4,128,128]{3,2,1,0:T(8,128)}, u32[]{:S(2)}, u32[]{:S(2)}) collective-permute-start(f32[2,4,128,128]{3,2,1,0:T(8,128)} %get-tuple-element.981), channel_id=1, source_target_pairs={{0,1},{1,2},{2,3},{3,4},{4,5},{5,6},{6,7},{7,8},{8,9},{9,10},{10,1... | collective-permute-start | bytes 1572872 | tf_op jit(solution)/shard_map/while/body/eval_jaxpr/ppermute | solution.py:21
  232.5 10.8 %collective-permute-start.3 = (f32[2,4,128,128]{3,2,1,0:T(8,128)}, f32[2,4,128,128]{3,2,1,0:T(8,128)S(1)}, u32[]{:S(2)}, u32[]{:S(2)}) collective-permute-start(f32[2,4,128,128]{3,2,1,0:T(8,128)} %get-tuple-element.984), channel_id=1, source_target_pairs={{1,0},{2,1},{3,2},{4,3},{5,4},{6,5},{7,6},{8,7},{9,8},{10,9},{11,1... | collective-permute-start | bytes 1572872 | tf_op jit(solution)/shard_map/while/body/eval_jaxpr/ppermute | solution.py:24
  245.9 1.2 copy-start.1
  247.5 1.0 copy-start.2
  249.5 13.8 %collective-permute-start.2 = (f32[2,4,128,128]{3,2,1,0:T(8,128)}, f32[2,4,128,128]{3,2,1,0:T(8,128)}, u32[]{:S(2)}, u32[]{:S(2)}) collective-permute-start(f32[2,4,128,128]{3,2,1,0:T(8,128)} %get-tuple-element.981), channel_id=1, source_target_pairs={{0,1},{1,2},{2,3},{3,4},{4,5},{5,6},{6,7},{7,8},{8,9},{9,10},{10,1... | collective-permute-start | bytes 1572872 | tf_op jit(solution)/shard_map/while/body/eval_jaxpr/ppermute | solution.py:21
  253.9 10.8 %collective-permute-start.3 = (f32[2,4,128,128]{3,2,1,0:T(8,128)}, f32[2,4,128,128]{3,2,1,0:T(8,128)S(1)}, u32[]{:S(2)}, u32[]{:S(2)}) collective-permute-start(f32[2,4,128,128]{3,2,1,0:T(8,128)} %get-tuple-element.984), channel_id=1, source_target_pairs={{1,0},{2,1},{3,2},{4,3},{5,4},{6,5},{7,6},{8,7},{9,8},{10,9},{11,1... | collective-permute-start | bytes 1572872 | tf_op jit(solution)/shard_map/while/body/eval_jaxpr/ppermute | solution.py:24
  267.2 1.2 copy-start.1
  268.8 1.0 copy-start.2
  269.8 10.9 %copy-start.5 = (f32[2,8,128,128]{3,2,1,0:T(8,128)S(1)}, f32[2,8,128,128]{3,2,1,0:T(8,128)}, u32[]{:S(2)}) copy-start(f32[2,8,128,128]{3,2,1,0:T(8,128)} %get-tuple-element.639) | copy-start | bytes 3145732
  269.8 40.6 %copy-start.6 = (s32[8]{0:T(128)S(1)}, s32[8]{0:T(128)}, u32[]{:S(2)}) copy-start(s32[8]{0:T(128)} %param.22) | copy-start | bytes 100
  272.7 33.0 %all-to-all-start.1 = ((f32[2,8,128,128]{3,1,0,2:T(8,128)}), f32[2,8,128,128]{3,1,0,2:T(8,128)S(1)}, u32[]{:S(2)}, u32[]{:S(2)}) async-start(f32[2,8,128,128]{3,1,0,2:T(8,128)} %copy.32), calls=%async_computation.1 | async-start | bytes 2097152 | tf_op jit(solution)/shard_map/all_to_all | solution.py:155
  305.6 29.7 %all-to-all-start = ((f32[2,8,128,128]{3,1,0,2:T(8,128)}), f32[2,8,128,128]{3,1,0,2:T(8,128)S(1)}, u32[]{:S(2)}, u32[]{:S(2)}) async-start(f32[2,8,128,128]{3,1,0,2:T(8,128)} %copy.29), calls=%async_computation | async-start | bytes 2097152 | tf_op jit(solution)/shard_map/all_to_all | solution.py:155
  (6 other events, 5.8 us)
where the time goes:
time: 349 us; the launch traced here: 346 us
  starting transfers between devices  87.6 us (25%)
  waiting for transfers between devices  77.2 us (22%)
  local copies, waits for them, and re-layouts  64.5 us (18%)
  other arithmetic  55.8 us (16%)
  loops' own time  31.6 us (9%)
  between operations  21.2 us (6%)
  matrix products  8.01 us (2%)
    ppermute x12, waiting for transfers between devices, extended_2(): lax.ppermute(lax.slice_in_dim(block, block.shape[dim] - width, None, axis...  52.2 us
    ppermute x12, starting transfers between devices, extended_2(): lax.ppermute(lax.slice_in_dim(block, block.shape[dim] - width, None, axis...  51.7 us
    while x84, local copies, waits for them, and re-layouts  33.2 us
    another operation x2, loops' own time, local(): lax.fori_loop(0, SNAP_EVERY, one_step, (current, previous, empty_snapshot))  31.6 us
    add x12, other arithmetic, advance(): updated = 2.0 * center - previous + speed_term * stencil(extended, layers)  29 us
    all_to_all x2, waiting for transfers between devices, local(): lax.all_to_all(snapshot, 'gz', split_axis=2, concat_axis=1, tiled=True)  24.8 us
    ppermute x12, starting transfers between devices, extended_2(): lax.ppermute(lax.slice_in_dim(block, 0, width, axis=dim), axis, backward)  23 us
    all_to_all x2, starting transfers between devices, local(): lax.all_to_all(snapshot, 'gz', split_axis=2, concat_axis=1, tiled=True)  12.8 us
  transfers between devices with their start and end apart: 26, of which 15 were waited for; matrix products, arithmetic and copies ran while one was open for 11% of the time, Pallas kernels for 0%

commit v1 on v0

--- a/solution.py
+++ b/solution.py
@@ -152,7 +152,9 @@
         current, previous, snapshot = lax.fori_loop(
             0, SNAP_EVERY, one_step, (current, previous, empty_snapshot)
         )
-        columns_now = lax.all_to_all(snapshot, "gz", split_axis=2, concat_axis=1, tiled=True)
+        out_arr = jnp.stack(jnp.split(snapshot, lax.axis_size("gz"), 2), axis=0)
+        met_up = lax.all_to_all(out_arr, "gz", 0, 0)
+        columns_now = jnp.concatenate(met_up, axis=1)
         raw_now, light_now = lag_images(columns_now, lag_offsets)
         if window == 0:
             raw_image = raw_now

time: 349 us -> 371 us (1.063)
  local copies, waits for them, and re-layouts: 64.5 us -> 92.7 us
  waiting for transfers between devices: 77.2 us -> 72.6 us
    unnamed x10 -> x42, local copies, waits for them, and re-layouts: 1.18 us -> 33.7 us
    all_to_all x2, waiting for transfers between devices: 24.8 us -> 18.1 us  [local(): met_up = lax.all_to_all(out_arr, 'gz', 0, 0)]
    while x86 -> x84, local copies, waits for them, and re-layouts: 37.7 us -> 33.1 us
  transfers between devices with their start and end apart: 26 -> 26, of which waited for: 15 -> 19; matrix products, arithmetic and copies ran while one was open for 11% -> 12% of each run, Pallas kernels for 0% -> 0%
where the time goes in v1:
time: 371 us; the launch traced here: 366 us
  local copies, waits for them, and re-layouts  92.7 us (25%)
  starting transfers between devices  87.2 us (24%)
  waiting for transfers between devices  72.6 us (20%)
  other arithmetic  55.8 us (15%)
  loops' own time  29.4 us (8%)
  between operations  20.7 us (6%)
  matrix products  8.01 us (2%)
    ppermute x12, waiting for transfers between devices, extended_2(): lax.ppermute(lax.slice_in_dim(block, block.shape[dim] - width, None, axis...  53.9 us
    ppermute x12, starting transfers between devices, extended_2(): lax.ppermute(lax.slice_in_dim(block, block.shape[dim] - width, None, axis...  51.3 us
    unnamed x42, local copies, waits for them, and re-layouts  33.7 us
    while x84, local copies, waits for them, and re-layouts  33.1 us
    another operation x2, loops' own time, local(): lax.fori_loop(0, SNAP_EVERY, one_step, (current, previous, empty_snapshot))  29.4 us
    add x12, other arithmetic, advance(): updated = 2.0 * center - previous + speed_term * stencil(extended, layers)  29 us
    ppermute x12, starting transfers between devices, extended_2(): lax.ppermute(lax.slice_in_dim(block, 0, width, axis=dim), axis, backward)  23 us
    all_to_all x2, waiting for transfers between devices, local(): met_up = lax.all_to_all(out_arr, 'gz', 0, 0)  18.1 us
  transfers between devices with their start and end apart: 26, of which 19 were waited for; matrix products, arithmetic and copies ran while one was open for 12% of the time, Pallas kernels for 0%

profile of v1, /device:TPU:9, one launch (start us, length us, event | category | flops | bytes accessed | tf_op | source)
XLA Modules:
  0.0 366.4 jit_solution(4616195983085457282)
XLA Ops:
  5.7 135.6 %while.44 = (s32[]{:T(128)}, f32[2,8,128,128]{3,2,1,0:T(8,128)S(1)}, f32[2,8,128,128]{3,2,1,0:T(8,128)S(1)}, f32[2,8,128,128]{3,2,1,0:T(8,128)}, s32[12]{0:T(128...) while((s32[]{:T(128)}, ...), condition=%wide.region_1.2_spmd.clone, body=%wide.region_0.1_spmd.clone.sunk | while | flops 24529312 | bytes 40568852 | solution.py:152
  6.7 3.7 %collective-permute-start = (f32[2,4,128,128]{3,2,1,0:T(8,128)}, f32[2,4,128,128]{3,2,1,0:T(8,128)}, u32[]{:S(2)}, u32[]{:S(2)}) collective-permute-start(f32[2,4,128,128]{3,2,1,0:T(8,128)} %get-tuple-element.925), channel_id=1, source_target_pairs={{0,1},{1,2},{2,3},{3,4},{4,5},{5,6},{6,7},{7,8},{8,9},{9,10},{10,1... | collective-permute-start | bytes 1572872 | tf_op jit(solution)/shard_map/while/body/eval_jaxpr/ppermute | solution.py:21
  10.5 1.9 collective-permute-start.1
  16.0 6.5 %collective-permute-done = f32[2,4,128,128]{3,2,1,0:T(8,128)} collective-permute-done((f32[2,4,128,128]{3,2,1,0:T(8,128)}, f32[2,4,128,128]{3,2,1,0:T(8,128)}, u32[]{:S(2)}, u32[]{:S(2)}) %collective-permute-start) | collective-permute-done | bytes 524320 | tf_op jit(solution)/shard_map/while/body/eval_jaxpr/ppermute | solution.py:21
  24.0 2.4 fusion.183
  30.1 4.3 %collective-permute-start = (f32[2,4,128,128]{3,2,1,0:T(8,128)}, f32[2,4,128,128]{3,2,1,0:T(8,128)}, u32[]{:S(2)}, u32[]{:S(2)}) collective-permute-start(f32[2,4,128,128]{3,2,1,0:T(8,128)} %get-tuple-element.925), channel_id=1, source_target_pairs={{0,1},{1,2},{2,3},{3,4},{4,5},{5,6},{6,7},{7,8},{8,9},{9,10},{10,1... | collective-permute-start | bytes 1572872 | tf_op jit(solution)/shard_map/while/body/eval_jaxpr/ppermute | solution.py:21
  34.3 1.9 collective-permute-start.1
  39.9 6.5 %collective-permute-done = f32[2,4,128,128]{3,2,1,0:T(8,128)} collective-permute-done((f32[2,4,128,128]{3,2,1,0:T(8,128)}, f32[2,4,128,128]{3,2,1,0:T(8,128)}, u32[]{:S(2)}, u32[]{:S(2)}) %collective-permute-start) | collective-permute-done | bytes 524320 | tf_op jit(solution)/shard_map/while/body/eval_jaxpr/ppermute | solution.py:21
  47.7 2.4 fusion.183
  53.8 4.4 %collective-permute-start = (f32[2,4,128,128]{3,2,1,0:T(8,128)}, f32[2,4,128,128]{3,2,1,0:T(8,128)}, u32[]{:S(2)}, u32[]{:S(2)}) collective-permute-start(f32[2,4,128,128]{3,2,1,0:T(8,128)} %get-tuple-element.925), channel_id=1, source_target_pairs={{0,1},{1,2},{2,3},{3,4},{4,5},{5,6},{6,7},{7,8},{8,9},{9,10},{10,1... | collective-permute-start | bytes 1572872 | tf_op jit(solution)/shard_map/while/body/eval_jaxpr/ppermute | solution.py:21
  58.2 1.9 collective-permute-start.1
  63.8 6.5 %collective-permute-done = f32[2,4,128,128]{3,2,1,0:T(8,128)} collective-permute-done((f32[2,4,128,128]{3,2,1,0:T(8,128)}, f32[2,4,128,128]{3,2,1,0:T(8,128)}, u32[]{:S(2)}, u32[]{:S(2)}) %collective-permute-start) | collective-permute-done | bytes 524320 | tf_op jit(solution)/shard_map/while/body/eval_jaxpr/ppermute | solution.py:21
  71.6 2.4 fusion.183
  77.7 4.4 %collective-permute-start = (f32[2,4,128,128]{3,2,1,0:T(8,128)}, f32[2,4,128,128]{3,2,1,0:T(8,128)}, u32[]{:S(2)}, u32[]{:S(2)}) collective-permute-start(f32[2,4,128,128]{3,2,1,0:T(8,128)} %get-tuple-element.925), channel_id=1, source_target_pairs={{0,1},{1,2},{2,3},{3,4},{4,5},{5,6},{6,7},{7,8},{8,9},{9,10},{10,1... | collective-permute-start | bytes 1572872 | tf_op jit(solution)/shard_map/while/body/eval_jaxpr/ppermute | solution.py:21
  82.1 1.9 collective-permute-start.1
  87.6 5.0 %collective-permute-done = f32[2,4,128,128]{3,2,1,0:T(8,128)} collective-permute-done((f32[2,4,128,128]{3,2,1,0:T(8,128)}, f32[2,4,128,128]{3,2,1,0:T(8,128)}, u32[]{:S(2)}, u32[]{:S(2)}) %collective-permute-start) | collective-permute-done | bytes 524320 | tf_op jit(solution)/shard_map/while/body/eval_jaxpr/ppermute | solution.py:21
  94.0 2.4 fusion.183
  100.0 4.4 %collective-permute-start = (f32[2,4,128,128]{3,2,1,0:T(8,128)}, f32[2,4,128,128]{3,2,1,0:T(8,128)}, u32[]{:S(2)}, u32[]{:S(2)}) collective-permute-start(f32[2,4,128,128]{3,2,1,0:T(8,128)} %get-tuple-element.925), channel_id=1, source_target_pairs={{0,1},{1,2},{2,3},{3,4},{4,5},{5,6},{6,7},{7,8},{8,9},{9,10},{10,1... | collective-permute-start | bytes 1572872 | tf_op jit(solution)/shard_map/while/body/eval_jaxpr/ppermute | solution.py:21
  104.4 1.9 collective-permute-start.1
  110.0 3.7 %collective-permute-done = f32[2,4,128,128]{3,2,1,0:T(8,128)} collective-permute-done((f32[2,4,128,128]{3,2,1,0:T(8,128)}, f32[2,4,128,128]{3,2,1,0:T(8,128)}, u32[]{:S(2)}, u32[]{:S(2)}) %collective-permute-start) | collective-permute-done | bytes 524320 | tf_op jit(solution)/shard_map/while/body/eval_jaxpr/ppermute | solution.py:21
  115.2 2.4 fusion.183
  121.3 4.3 %collective-permute-start = (f32[2,4,128,128]{3,2,1,0:T(8,128)}, f32[2,4,128,128]{3,2,1,0:T(8,128)}, u32[]{:S(2)}, u32[]{:S(2)}) collective-permute-start(f32[2,4,128,128]{3,2,1,0:T(8,128)} %get-tuple-element.925), channel_id=1, source_target_pairs={{0,1},{1,2},{2,3},{3,4},{4,5},{5,6},{6,7},{7,8},{8,9},{9,10},{10,1... | collective-permute-start | bytes 1572872 | tf_op jit(solution)/shard_map/while/body/eval_jaxpr/ppermute | solution.py:21
  125.5 1.9 collective-permute-start.1
  131.1 3.8 %collective-permute-done = f32[2,4,128,128]{3,2,1,0:T(8,128)} collective-permute-done((f32[2,4,128,128]{3,2,1,0:T(8,128)}, f32[2,4,128,128]{3,2,1,0:T(8,128)}, u32[]{:S(2)}, u32[]{:S(2)}) %collective-permute-start) | collective-permute-done | bytes 524320 | tf_op jit(solution)/shard_map/while/body/eval_jaxpr/ppermute | solution.py:21
  136.3 2.4 fusion.183
  141.3 127.6 %while.45 = (s32[]{:T(128)}, f32[2,8,128,128]{3,2,1,0:T(8,128)S(1)}, f32[2,8,128,128]{3,2,1,0:T(8,128)S(1)}, f32[2,8,128,128]{3,2,1,0:T(8,128)}, s32[12]{0:T(128...) while((s32[]{:T(128)}, ...), condition=%wide.region_3.4_spmd.clone, body=%wide.region_2.3_spmd.clone.sunk | while | flops 24529316 | bytes 40568908 | solution.py:152
  142.4 4.4 %collective-permute-start.2 = (f32[2,4,128,128]{3,2,1,0:T(8,128)}, f32[2,4,128,128]{3,2,1,0:T(8,128)}, u32[]{:S(2)}, u32[]{:S(2)}) collective-permute-start(f32[2,4,128,128]{3,2,1,0:T(8,128)} %get-tuple-element.941), channel_id=1, source_target_pairs={{0,1},{1,2},{2,3},{3,4},{4,5},{5,6},{6,7},{7,8},{8,9},{9,10},{10,1... | collective-permute-start | bytes 1572872 | tf_op jit(solution)/shard_map/while/body/eval_jaxpr/ppermute | solution.py:21
  152.5 3.5 collective-permute-done.2
  157.5 2.4 fusion.188
  163.6 4.3 %collective-permute-start.2 = (f32[2,4,128,128]{3,2,1,0:T(8,128)}, f32[2,4,128,128]{3,2,1,0:T(8,128)}, u32[]{:S(2)}, u32[]{:S(2)}) collective-permute-start(f32[2,4,128,128]{3,2,1,0:T(8,128)} %get-tuple-element.941), channel_id=1, source_target_pairs={{0,1},{1,2},{2,3},{3,4},{4,5},{5,6},{6,7},{7,8},{8,9},{9,10},{10,1... | collective-permute-start | bytes 1572872 | tf_op jit(solution)/shard_map/while/body/eval_jaxpr/ppermute | solution.py:21
  173.6 3.8 %collective-permute-done.2 = f32[2,4,128,128]{3,2,1,0:T(8,128)} collective-permute-done((f32[2,4,128,128]{3,2,1,0:T(8,128)}, f32[2,4,128,128]{3,2,1,0:T(8,128)}, u32[]{:S(2)}, u32[]{:S(2)}) %collective-permute-start.2) | collective-permute-done | bytes 524320 | tf_op jit(solution)/shard_map/while/body/eval_jaxpr/ppermute | solution.py:21
  178.8 2.4 fusion.188
  184.9 4.4 %collective-permute-start.2 = (f32[2,4,128,128]{3,2,1,0:T(8,128)}, f32[2,4,128,128]{3,2,1,0:T(8,128)}, u32[]{:S(2)}, u32[]{:S(2)}) collective-permute-start(f32[2,4,128,128]{3,2,1,0:T(8,128)} %get-tuple-element.941), channel_id=1, source_target_pairs={{0,1},{1,2},{2,3},{3,4},{4,5},{5,6},{6,7},{7,8},{8,9},{9,10},{10,1... | collective-permute-start | bytes 1572872 | tf_op jit(solution)/shard_map/while/body/eval_jaxpr/ppermute | solution.py:21
  195.1 3.5 collective-permute-done.2
  200.0 2.4 fusion.188
  206.1 4.3 %collective-permute-start.2 = (f32[2,4,128,128]{3,2,1,0:T(8,128)}, f32[2,4,128,128]{3,2,1,0:T(8,128)}, u32[]{:S(2)}, u32[]{:S(2)}) collective-permute-start(f32[2,4,128,128]{3,2,1,0:T(8,128)} %get-tuple-element.941), channel_id=1, source_target_pairs={{0,1},{1,2},{2,3},{3,4},{4,5},{5,6},{6,7},{7,8},{8,9},{9,10},{10,1... | collective-permute-start | bytes 1572872 | tf_op jit(solution)/shard_map/while/body/eval_jaxpr/ppermute | solution.py:21
  216.2 3.8 %collective-permute-done.2 = f32[2,4,128,128]{3,2,1,0:T(8,128)} collective-permute-done((f32[2,4,128,128]{3,2,1,0:T(8,128)}, f32[2,4,128,128]{3,2,1,0:T(8,128)}, u32[]{:S(2)}, u32[]{:S(2)}) %collective-permute-start.2) | collective-permute-done | bytes 524320 | tf_op jit(solution)/shard_map/while/body/eval_jaxpr/ppermute | solution.py:21
  221.4 2.4 fusion.188
  227.5 4.4 %collective-permute-start.2 = (f32[2,4,128,128]{3,2,1,0:T(8,128)}, f32[2,4,128,128]{3,2,1,0:T(8,128)}, u32[]{:S(2)}, u32[]{:S(2)}) collective-permute-start(f32[2,4,128,128]{3,2,1,0:T(8,128)} %get-tuple-element.941), channel_id=1, source_target_pairs={{0,1},{1,2},{2,3},{3,4},{4,5},{5,6},{6,7},{7,8},{8,9},{9,10},{10,1... | collective-permute-start | bytes 1572872 | tf_op jit(solution)/shard_map/while/body/eval_jaxpr/ppermute | solution.py:21
  237.6 3.5 collective-permute-done.2
  242.6 2.4 fusion.188
  248.7 4.3 %collective-permute-start.2 = (f32[2,4,128,128]{3,2,1,0:T(8,128)}, f32[2,4,128,128]{3,2,1,0:T(8,128)}, u32[]{:S(2)}, u32[]{:S(2)}) collective-permute-start(f32[2,4,128,128]{3,2,1,0:T(8,128)} %get-tuple-element.941), channel_id=1, source_target_pairs={{0,1},{1,2},{2,3},{3,4},{4,5},{5,6},{6,7},{7,8},{8,9},{9,10},{10,1... | collective-permute-start | bytes 1572872 | tf_op jit(solution)/shard_map/while/body/eval_jaxpr/ppermute | solution.py:21
  258.7 3.8 %collective-permute-done.2 = f32[2,4,128,128]{3,2,1,0:T(8,128)} collective-permute-done((f32[2,4,128,128]{3,2,1,0:T(8,128)}, f32[2,4,128,128]{3,2,1,0:T(8,128)}, u32[]{:S(2)}, u32[]{:S(2)}) %collective-permute-start.2) | collective-permute-done | bytes 524320 | tf_op jit(solution)/shard_map/while/body/eval_jaxpr/ppermute | solution.py:21
  263.9 2.4 fusion.188
  292.4 8.1 %all-to-all-start.1 = ((f32[16,2,8,8,128]{4,3,2,1,0:T(8,128)}), f32[16,2,8,8,128]{4,3,2,1,0:T(8,128)S(1)}, u32[]{:S(2)}, u32[]{:S(2)}) async-start(f32[16,2,8,8,128]{4,3,2,1,0:T(8,128)} %constant_dynamic-update-slice_fusion.24), calls=%async_computation.1 | async-start | bytes 2097152 | tf_op jit(solution)/shard_map/all_to_all | solution.py:156
  310.8 14.7 %all-to-all-done.1 = f32[16,2,8,8,128]{4,3,2,1,0:T(8,128)S(1)} async-done(((f32[16,2,8,8,128]{4,3,2,1,0:T(8,128)}), f32[16,2,8,8,128]{4,3,2,1,0:T(8,128)S(1)}, u32[]{:S(2)}, u32[]{:S(2)}) %all-to-all-start.1) | async-done | bytes 1048608 | tf_op jit(solution)/shard_map/all_to_all | solution.py:156
  325.5 4.8 %all-to-all-start = ((f32[16,2,8,8,128]{4,3,2,1,0:T(8,128)}), f32[16,2,8,8,128]{4,3,2,1,0:T(8,128)S(1)}, u32[]{:S(2)}, u32[]{:S(2)}) async-start(f32[16,2,8,8,128]{4,3,2,1,0:T(8,128)} %constant_dynamic-update-slice_fusion.8), calls=%async_computation | async-start | bytes 2097152 | tf_op jit(solution)/shard_map/all_to_all | solution.py:156
  351.8 3.4 all-to-all-done
  (305 shorter events, 139.7 us)
Async XLA Ops:
  0.6 5.0 %copy-start.8 = (s32[12]{0:T(128)S(1)}, s32[12]{0:T(128)}, u32[]{:S(2)}) copy-start(s32[12]{0:T(128)} %param.20) | copy-start | bytes 148
  0.6 5.0 %copy-start = (f32[8,128,128]{2,1,0:T(8,128)S(1)}, f32[8,128,128]{2,1,0:T(8,128)}, u32[]{:S(2)}) copy-start(f32[8,128,128]{2,1,0:T(8,128)} %param.18) | copy-start | bytes 1572868
  6.7 15.7 %collective-permute-start = (f32[2,4,128,128]{3,2,1,0:T(8,128)}, f32[2,4,128,128]{3,2,1,0:T(8,128)}, u32[]{:S(2)}, u32[]{:S(2)}) collective-permute-start(f32[2,4,128,128]{3,2,1,0:T(8,128)} %get-tuple-element.925), channel_id=1, source_target_pairs={{0,1},{1,2},{2,3},{3,4},{4,5},{5,6},{6,7},{7,8},{8,9},{9,10},{10,1... | collective-permute-start | bytes 1572872 | tf_op jit(solution)/shard_map/while/body/eval_jaxpr/ppermute | solution.py:21
  10.5 13.5 %collective-permute-start.1 = (f32[2,4,128,128]{3,2,1,0:T(8,128)}, f32[2,4,128,128]{3,2,1,0:T(8,128)S(1)}, u32[]{:S(2)}, u32[]{:S(2)}) collective-permute-start(f32[2,4,128,128]{3,2,1,0:T(8,128)} %get-tuple-element.928), channel_id=1, source_target_pairs={{1,0},{2,1},{3,2},{4,3},{5,4},{6,5},{7,6},{8,7},{9,8},{10,9},{11,1... | collective-permute-start | bytes 1572872 | tf_op jit(solution)/shard_map/while/body/eval_jaxpr/ppermute | solution.py:24
  26.4 1.2 copy-start.3
  30.1 16.3 %collective-permute-start = (f32[2,4,128,128]{3,2,1,0:T(8,128)}, f32[2,4,128,128]{3,2,1,0:T(8,128)}, u32[]{:S(2)}, u32[]{:S(2)}) collective-permute-start(f32[2,4,128,128]{3,2,1,0:T(8,128)} %get-tuple-element.925), channel_id=1, source_target_pairs={{0,1},{1,2},{2,3},{3,4},{4,5},{5,6},{6,7},{7,8},{8,9},{9,10},{10,1... | collective-permute-start | bytes 1572872 | tf_op jit(solution)/shard_map/while/body/eval_jaxpr/ppermute | solution.py:21
  34.3 13.4 %collective-permute-start.1 = (f32[2,4,128,128]{3,2,1,0:T(8,128)}, f32[2,4,128,128]{3,2,1,0:T(8,128)S(1)}, u32[]{:S(2)}, u32[]{:S(2)}) collective-permute-start(f32[2,4,128,128]{3,2,1,0:T(8,128)} %get-tuple-element.928), channel_id=1, source_target_pairs={{1,0},{2,1},{3,2},{4,3},{5,4},{6,5},{7,6},{8,7},{9,8},{10,9},{11,1... | collective-permute-start | bytes 1572872 | tf_op jit(solution)/shard_map/while/body/eval_jaxpr/ppermute | solution.py:24
  50.2 1.2 copy-start.3
  53.8 16.4 %collective-permute-start = (f32[2,4,128,128]{3,2,1,0:T(8,128)}, f32[2,4,128,128]{3,2,1,0:T(8,128)}, u32[]{:S(2)}, u32[]{:S(2)}) collective-permute-start(f32[2,4,128,128]{3,2,1,0:T(8,128)} %get-tuple-element.925), channel_id=1, source_target_pairs={{0,1},{1,2},{2,3},{3,4},{4,5},{5,6},{6,7},{7,8},{8,9},{9,10},{10,1... | collective-permute-start | bytes 1572872 | tf_op jit(solution)/shard_map/while/body/eval_jaxpr/ppermute | solution.py:21
  58.2 13.4 %collective-permute-start.1 = (f32[2,4,128,128]{3,2,1,0:T(8,128)}, f32[2,4,128,128]{3,2,1,0:T(8,128)S(1)}, u32[]{:S(2)}, u32[]{:S(2)}) collective-permute-start(f32[2,4,128,128]{3,2,1,0:T(8,128)} %get-tuple-element.928), channel_id=1, source_target_pairs={{1,0},{2,1},{3,2},{4,3},{5,4},{6,5},{7,6},{8,7},{9,8},{10,9},{11,1... | collective-permute-start | bytes 1572872 | tf_op jit(solution)/shard_map/while/body/eval_jaxpr/ppermute | solution.py:24
  74.0 1.2 copy-start.3
  77.7 14.9 %collective-permute-start = (f32[2,4,128,128]{3,2,1,0:T(8,128)}, f32[2,4,128,128]{3,2,1,0:T(8,128)}, u32[]{:S(2)}, u32[]{:S(2)}) collective-permute-start(f32[2,4,128,128]{3,2,1,0:T(8,128)} %get-tuple-element.925), channel_id=1, source_target_pairs={{0,1},{1,2},{2,3},{3,4},{4,5},{5,6},{6,7},{7,8},{8,9},{9,10},{10,1... | collective-permute-start | bytes 1572872 | tf_op jit(solution)/shard_map/while/body/eval_jaxpr/ppermute | solution.py:21
  82.1 11.8 %collective-permute-start.1 = (f32[2,4,128,128]{3,2,1,0:T(8,128)}, f32[2,4,128,128]{3,2,1,0:T(8,128)S(1)}, u32[]{:S(2)}, u32[]{:S(2)}) collective-permute-start(f32[2,4,128,128]{3,2,1,0:T(8,128)} %get-tuple-element.928), channel_id=1, source_target_pairs={{1,0},{2,1},{3,2},{4,3},{5,4},{6,5},{7,6},{8,7},{9,8},{10,9},{11,1... | collective-permute-start | bytes 1572872 | tf_op jit(solution)/shard_map/while/body/eval_jaxpr/ppermute | solution.py:24
  96.4 1.2 copy-start.3
  100.0 13.6 %collective-permute-start = (f32[2,4,128,128]{3,2,1,0:T(8,128)}, f32[2,4,128,128]{3,2,1,0:T(8,128)}, u32[]{:S(2)}, u32[]{:S(2)}) collective-permute-start(f32[2,4,128,128]{3,2,1,0:T(8,128)} %get-tuple-element.925), channel_id=1, source_target_pairs={{0,1},{1,2},{2,3},{3,4},{4,5},{5,6},{6,7},{7,8},{8,9},{9,10},{10,1... | collective-permute-start | bytes 1572872 | tf_op jit(solution)/shard_map/while/body/eval_jaxpr/ppermute | solution.py:21
  104.4 10.7 %collective-permute-start.1 = (f32[2,4,128,128]{3,2,1,0:T(8,128)}, f32[2,4,128,128]{3,2,1,0:T(8,128)S(1)}, u32[]{:S(2)}, u32[]{:S(2)}) collective-permute-start(f32[2,4,128,128]{3,2,1,0:T(8,128)} %get-tuple-element.928), channel_id=1, source_target_pairs={{1,0},{2,1},{3,2},{4,3},{5,4},{6,5},{7,6},{8,7},{9,8},{10,9},{11,1... | collective-permute-start | bytes 1572872 | tf_op jit(solution)/shard_map/while/body/eval_jaxpr/ppermute | solution.py:24
  117.6 1.2 copy-start.3
  121.3 13.6 %collective-permute-start = (f32[2,4,128,128]{3,2,1,0:T(8,128)}, f32[2,4,128,128]{3,2,1,0:T(8,128)}, u32[]{:S(2)}, u32[]{:S(2)}) collective-permute-start(f32[2,4,128,128]{3,2,1,0:T(8,128)} %get-tuple-element.925), channel_id=1, source_target_pairs={{0,1},{1,2},{2,3},{3,4},{4,5},{5,6},{6,7},{7,8},{8,9},{9,10},{10,1... | collective-permute-start | bytes 1572872 | tf_op jit(solution)/shard_map/while/body/eval_jaxpr/ppermute | solution.py:21
  125.5 10.7 %collective-permute-start.1 = (f32[2,4,128,128]{3,2,1,0:T(8,128)}, f32[2,4,128,128]{3,2,1,0:T(8,128)S(1)}, u32[]{:S(2)}, u32[]{:S(2)}) collective-permute-start(f32[2,4,128,128]{3,2,1,0:T(8,128)} %get-tuple-element.928), channel_id=1, source_target_pairs={{1,0},{2,1},{3,2},{4,3},{5,4},{6,5},{7,6},{8,7},{9,8},{10,9},{11,1... | collective-permute-start | bytes 1572872 | tf_op jit(solution)/shard_map/while/body/eval_jaxpr/ppermute | solution.py:24
  138.7 1.2 copy-start.3
  142.4 13.6 %collective-permute-start.2 = (f32[2,4,128,128]{3,2,1,0:T(8,128)}, f32[2,4,128,128]{3,2,1,0:T(8,128)}, u32[]{:S(2)}, u32[]{:S(2)}) collective-permute-start(f32[2,4,128,128]{3,2,1,0:T(8,128)} %get-tuple-element.941), channel_id=1, source_target_pairs={{0,1},{1,2},{2,3},{3,4},{4,5},{5,6},{6,7},{7,8},{8,9},{9,10},{10,1... | collective-permute-start | bytes 1572872 | tf_op jit(solution)/shard_map/while/body/eval_jaxpr/ppermute | solution.py:21
  146.7 10.7 %collective-permute-start.3 = (f32[2,4,128,128]{3,2,1,0:T(8,128)}, f32[2,4,128,128]{3,2,1,0:T(8,128)S(1)}, u32[]{:S(2)}, u32[]{:S(2)}) collective-permute-start(f32[2,4,128,128]{3,2,1,0:T(8,128)} %get-tuple-element.944), channel_id=1, source_target_pairs={{1,0},{2,1},{3,2},{4,3},{5,4},{6,5},{7,6},{8,7},{9,8},{10,9},{11,1... | collective-permute-start | bytes 1572872 | tf_op jit(solution)/shard_map/while/body/eval_jaxpr/ppermute | solution.py:24
  159.9 1.2 copy-start.1
  161.5 1.0 copy-start.2
  163.6 13.9 %collective-permute-start.2 = (f32[2,4,128,128]{3,2,1,0:T(8,128)}, f32[2,4,128,128]{3,2,1,0:T(8,128)}, u32[]{:S(2)}, u32[]{:S(2)}) collective-permute-start(f32[2,4,128,128]{3,2,1,0:T(8,128)} %get-tuple-element.941), channel_id=1, source_target_pairs={{0,1},{1,2},{2,3},{3,4},{4,5},{5,6},{6,7},{7,8},{8,9},{9,10},{10,1... | collective-permute-start | bytes 1572872 | tf_op jit(solution)/shard_map/while/body/eval_jaxpr/ppermute | solution.py:21
  167.9 10.9 %collective-permute-start.3 = (f32[2,4,128,128]{3,2,1,0:T(8,128)}, f32[2,4,128,128]{3,2,1,0:T(8,128)S(1)}, u32[]{:S(2)}, u32[]{:S(2)}) collective-permute-start(f32[2,4,128,128]{3,2,1,0:T(8,128)} %get-tuple-element.944), channel_id=1, source_target_pairs={{1,0},{2,1},{3,2},{4,3},{5,4},{6,5},{7,6},{8,7},{9,8},{10,9},{11,1... | collective-permute-start | bytes 1572872 | tf_op jit(solution)/shard_map/while/body/eval_jaxpr/ppermute | solution.py:24
  181.2 1.2 copy-start.1
  182.9 1.0 copy-start.2
  184.9 13.6 %collective-permute-start.2 = (f32[2,4,128,128]{3,2,1,0:T(8,128)}, f32[2,4,128,128]{3,2,1,0:T(8,128)}, u32[]{:S(2)}, u32[]{:S(2)}) collective-permute-start(f32[2,4,128,128]{3,2,1,0:T(8,128)} %get-tuple-element.941), channel_id=1, source_target_pairs={{0,1},{1,2},{2,3},{3,4},{4,5},{5,6},{6,7},{7,8},{8,9},{9,10},{10,1... | collective-permute-start | bytes 1572872 | tf_op jit(solution)/shard_map/while/body/eval_jaxpr/ppermute | solution.py:21
  189.3 10.7 %collective-permute-start.3 = (f32[2,4,128,128]{3,2,1,0:T(8,128)}, f32[2,4,128,128]{3,2,1,0:T(8,128)S(1)}, u32[]{:S(2)}, u32[]{:S(2)}) collective-permute-start(f32[2,4,128,128]{3,2,1,0:T(8,128)} %get-tuple-element.944), channel_id=1, source_target_pairs={{1,0},{2,1},{3,2},{4,3},{5,4},{6,5},{7,6},{8,7},{9,8},{10,9},{11,1... | collective-permute-start | bytes 1572872 | tf_op jit(solution)/shard_map/while/body/eval_jaxpr/ppermute | solution.py:24
  202.5 1.2 copy-start.1
  204.1 1.0 copy-start.2
  206.1 13.9 %collective-permute-start.2 = (f32[2,4,128,128]{3,2,1,0:T(8,128)}, f32[2,4,128,128]{3,2,1,0:T(8,128)}, u32[]{:S(2)}, u32[]{:S(2)}) collective-permute-start(f32[2,4,128,128]{3,2,1,0:T(8,128)} %get-tuple-element.941), channel_id=1, source_target_pairs={{0,1},{1,2},{2,3},{3,4},{4,5},{5,6},{6,7},{7,8},{8,9},{9,10},{10,1... | collective-permute-start | bytes 1572872 | tf_op jit(solution)/shard_map/while/body/eval_jaxpr/ppermute | solution.py:21
  210.4 10.9 %collective-permute-start.3 = (f32[2,4,128,128]{3,2,1,0:T(8,128)}, f32[2,4,128,128]{3,2,1,0:T(8,128)S(1)}, u32[]{:S(2)}, u32[]{:S(2)}) collective-permute-start(f32[2,4,128,128]{3,2,1,0:T(8,128)} %get-tuple-element.944), channel_id=1, source_target_pairs={{1,0},{2,1},{3,2},{4,3},{5,4},{6,5},{7,6},{8,7},{9,8},{10,9},{11,1... | collective-permute-start | bytes 1572872 | tf_op jit(solution)/shard_map/while/body/eval_jaxpr/ppermute | solution.py:24
  223.8 1.2 copy-start.1
  225.4 1.0 copy-start.2
  227.5 13.6 %collective-permute-start.2 = (f32[2,4,128,128]{3,2,1,0:T(8,128)}, f32[2,4,128,128]{3,2,1,0:T(8,128)}, u32[]{:S(2)}, u32[]{:S(2)}) collective-permute-start(f32[2,4,128,128]{3,2,1,0:T(8,128)} %get-tuple-element.941), channel_id=1, source_target_pairs={{0,1},{1,2},{2,3},{3,4},{4,5},{5,6},{6,7},{7,8},{8,9},{9,10},{10,1... | collective-permute-start | bytes 1572872 | tf_op jit(solution)/shard_map/while/body/eval_jaxpr/ppermute | solution.py:21
  231.8 10.7 %collective-permute-start.3 = (f32[2,4,128,128]{3,2,1,0:T(8,128)}, f32[2,4,128,128]{3,2,1,0:T(8,128)S(1)}, u32[]{:S(2)}, u32[]{:S(2)}) collective-permute-start(f32[2,4,128,128]{3,2,1,0:T(8,128)} %get-tuple-element.944), channel_id=1, source_target_pairs={{1,0},{2,1},{3,2},{4,3},{5,4},{6,5},{7,6},{8,7},{9,8},{10,9},{11,1... | collective-permute-start | bytes 1572872 | tf_op jit(solution)/shard_map/while/body/eval_jaxpr/ppermute | solution.py:24
  245.0 1.2 copy-start.1
  246.6 1.0 copy-start.2
  248.7 13.9 %collective-permute-start.2 = (f32[2,4,128,128]{3,2,1,0:T(8,128)}, f32[2,4,128,128]{3,2,1,0:T(8,128)}, u32[]{:S(2)}, u32[]{:S(2)}) collective-permute-start(f32[2,4,128,128]{3,2,1,0:T(8,128)} %get-tuple-element.941), channel_id=1, source_target_pairs={{0,1},{1,2},{2,3},{3,4},{4,5},{5,6},{6,7},{7,8},{8,9},{9,10},{10,1... | collective-permute-start | bytes 1572872 | tf_op jit(solution)/shard_map/while/body/eval_jaxpr/ppermute | solution.py:21
  253.0 10.9 %collective-permute-start.3 = (f32[2,4,128,128]{3,2,1,0:T(8,128)}, f32[2,4,128,128]{3,2,1,0:T(8,128)S(1)}, u32[]{:S(2)}, u32[]{:S(2)}) collective-permute-start(f32[2,4,128,128]{3,2,1,0:T(8,128)} %get-tuple-element.944), channel_id=1, source_target_pairs={{1,0},{2,1},{3,2},{4,3},{5,4},{6,5},{7,6},{8,7},{9,8},{10,9},{11,1... | collective-permute-start | bytes 1572872 | tf_op jit(solution)/shard_map/while/body/eval_jaxpr/ppermute | solution.py:24
  266.3 1.2 copy-start.1
  267.9 1.0 copy-start.2
  268.9 31.7 %copy-start.5 = (f32[2,8,128,128]{3,2,1,0:T(8,128)S(1)}, f32[2,8,128,128]{3,2,1,0:T(8,128)}, u32[]{:S(2)}) copy-start(f32[2,8,128,128]{3,2,1,0:T(8,128)} %get-tuple-element.639) | copy-start | bytes 3145732
  268.9 61.3 %copy-start.7 = (s32[8]{0:T(128)S(1)}, s32[8]{0:T(128)}, u32[]{:S(2)}) copy-start(s32[8]{0:T(128)} %param.22) | copy-start | bytes 100
  292.4 33.1 %all-to-all-start.1 = ((f32[16,2,8,8,128]{4,3,2,1,0:T(8,128)}), f32[16,2,8,8,128]{4,3,2,1,0:T(8,128)S(1)}, u32[]{:S(2)}, u32[]{:S(2)}) async-start(f32[16,2,8,8,128]{4,3,2,1,0:T(8,128)} %constant_dynamic-update-slice_fusion.24), calls=%async_computation.1 | async-start | bytes 2097152 | tf_op jit(solution)/shard_map/all_to_all | solution.py:156
  325.5 29.7 %all-to-all-start = ((f32[16,2,8,8,128]{4,3,2,1,0:T(8,128)}), f32[16,2,8,8,128]{4,3,2,1,0:T(8,128)S(1)}, u32[]{:S(2)}, u32[]{:S(2)}) async-start(f32[16,2,8,8,128]{4,3,2,1,0:T(8,128)} %constant_dynamic-update-slice_fusion.8), calls=%async_computation | async-start | bytes 2097152 | tf_op jit(solution)/shard_map/all_to_all | solution.py:156
  (7 other events, 6.8 us)
